TPU v7x, 512 devices: a whole 4x8x8 slice. The times are simulated.
512 devices in a mesh: tm: 32 (over z, y_lo, core), depth: 16 (over x, y_hi).
Axes of the slice: x: 4, y: 8 (y_hi: 4, y_lo: 2; y = y_hi * 2 + y_lo), z: 8, core: 2. Of those that a mesh axis runs over, the one named last changes fastest.
Arguments:
- raw: bfloat16 [512, 128, 128], P('tm', 'depth'), may hold values from -6 to 6
- stream: bfloat16 [512, 128, 2048], P('tm', 'depth'), may hold values from -6 to 6
- conv_w: bfloat16 [3, 128, 2048], replicated, may hold values from -0.3125 to 0.3125
- gain: float32 [2048], replicated, may hold values from 0.1 to 1.9
- w_qkv: bfloat16 [2048, 3072], P('tm', 'depth'), may hold values from -4 to 4
- mask: int32 [16, 32, 5], P('depth', 'tm'), may hold values from 0 to 1, as said below
Outputs:
- context: bfloat16 [512, 128, 1024], P('tm', 'depth')
Inputs may be any that keep to these rules, and one draw needn't show every extreme that they name: mask[p, i, 2] = 1 for every block; mask[p, i, e] = 0 wherever i + e - 2 lies outside 0 to 31.
All inputs are finite; a program needn't handle non-finite values.
Results may differ from a plain program's by a relative error of at most 0.012.
The roundings to bfloat16 on the way count: a program that leaves them out, or rounds other values in their place, can miss the bound.
Values may be sent and summed in bfloat16 or wider, within the bound.
A program may use at most 64 MiB of HBM per device.

v0:
```python
import math
import jax
import jax.numpy as jnp
from jax import lax
from jax.sharding import PartitionSpec as P

HEADS = 8
HD = 128
BT = 16
PP = 8
RD = 2


def padded_2(value, sides, width):
    for axis, dim in sides:
        devices, length = (lax.axis_size(axis), value.shape[dim])
        up = [(i, (i + 1) % devices) for i in range(devices - 1)]
        down = [(j, i) for i, j in up]
        last = lax.slice_in_dim(value, length - width, length, axis=dim)
        leading = lax.slice_in_dim(value, 0, width, axis=dim)
        before = lax.ppermute(last, axis, up)
        after = lax.ppermute(leading, axis, down)
        value = jnp.concatenate([before, value, after], axis=dim)
    return value


def from_behind(value, axis, by):
    devices = lax.axis_size(axis)
    pairs = [(i, i + by) for i in range(devices) if 0 <= i + by < devices]
    return lax.ppermute(value, axis, pairs)


def head_attend(query_head, key_head, value_head, allowed):
    inv_root = 1.0 / math.sqrt(HD)
    scores = (
        jnp.einsum("qd,kd->qk", query_head, key_head, preferred_element_type=jnp.float32) * inv_root
    )
    scores = jnp.where(allowed, scores, -1e30)
    row_max = jnp.max(scores, axis=-1, keepdims=True)
    powers = jnp.exp(scores - row_max)
    weights = (powers / jnp.sum(powers, axis=-1, keepdims=True)).astype(jnp.bfloat16)
    return jnp.dot(weights, value_head, preferred_element_type=jnp.float32).astype(jnp.bfloat16)


def per_device(raw, stream, conv_w, gain, w_qkv, mask):
    time_len, site_len, feat_len = raw.shape
    tok_rows = time_len * site_len
    padded = padded_2(raw, (("depth", 1),), 1)
    embedded = stream.reshape(tok_rows, stream.shape[2]).astype(jnp.float32)
    for offset in range(3):
        window = padded[:, offset : offset + site_len].reshape(tok_rows, feat_len)
        embedded = embedded + jnp.dot(window, conv_w[offset], preferred_element_type=jnp.float32)
    normed = (
        embedded * lax.rsqrt(jnp.mean(embedded * embedded, axis=-1, keepdims=True) + 1e-05) * gain
    ).astype(jnp.bfloat16)
    columns = lax.all_gather(w_qkv, "depth", axis=1, tiled=True)
    projected = jnp.dot(
        normed,
        lax.all_gather(columns, "tm", axis=0, tiled=True),
        preferred_element_type=jnp.float32,
    ).astype(jnp.bfloat16)
    head_cols = projected.shape[1] // 3
    queries = projected[:, :head_cols]
    keyvals = projected[:, head_cols:]
    earlier = []
    later = []
    moving_back = keyvals
    moving_ahead = keyvals
    for hop_index in range(RD):
        moving_back = from_behind(moving_back, "tm", 1)
        moving_ahead = from_behind(moving_ahead, "tm", -1)
        earlier.insert(0, moving_back)
        later.append(moving_ahead)
    gathered = jnp.concatenate(earlier + [keyvals] + later, axis=0)
    block_rows = BT * PP
    own_blocks = tok_rows // block_rows
    span_blocks = gathered.shape[0] // block_rows
    local_mask = mask[0]
    query_ids = jnp.arange(own_blocks, dtype=jnp.int32)[:, None]
    key_ids = jnp.arange(span_blocks, dtype=jnp.int32)[None, :]
    entry_ids = key_ids - query_ids
    picks = entry_ids[:, :, None] == jnp.arange(local_mask.shape[1], dtype=jnp.int32)[None, None, :]
    block_allowed = jnp.sum(jnp.where(picks, local_mask[:, None, :], 0), axis=-1) > 0
    allowed = jnp.repeat(jnp.repeat(block_allowed, block_rows, axis=0), block_rows, axis=1)
    query_heads = queries.reshape(tok_rows, HEADS, HD).transpose(1, 0, 2)
    key_heads = gathered[:, :head_cols].reshape(gathered.shape[0], HEADS, HD).transpose(1, 0, 2)
    value_heads = gathered[:, head_cols:].reshape(gathered.shape[0], HEADS, HD).transpose(1, 0, 2)
    context = lax.map(
        lambda operands: head_attend(operands[0], operands[1], operands[2], allowed),
        (query_heads, key_heads, value_heads),
    )
    return context.transpose(1, 0, 2).reshape(time_len, site_len, head_cols)


def solution(mesh):
    in_specs = (
        P("tm", "depth", None),
        P("tm", "depth", None),
        P(),
        P(),
        P("tm", "depth"),
        P("depth", "tm", None),
    )
    out_specs = P("tm", "depth", None)
    return jax.shard_map(
        per_device, mesh=mesh, in_specs=in_specs, out_specs=out_specs, check_vma=False
    )
```

profile of v0, /device:TPU:1, one launch (start us, length us, event | category | flops | bytes accessed | tf_op | source)
XLA Modules:
  0.0 192.2 jit_solution(5119026603187726884)
XLA Ops:
  6.5 42.6 %all-gather = bf16[16,192,64]{1,2,0:T(8,128)(2,1)S(1)} all-gather(bf16[1,192,64]{1,2,0:T(8,128)(2,1)} %bitcast.82), channel_id=1, replica_groups=mesh['tm'=32,'depth'=16] {'depth'}, dimensions={0}, use_global_device_ids=true | all-gather | bytes 417792 | tf_op jit(solution)/shard_map/all_gather | solution.py:56
  49.4 1.3 reshape.102
  50.8 1.3 collective-permute-start
  52.1 1.3 collective-permute-start.1
  54.0 3.4 %collective-permute-done.1 = bf16[16,1,128]{2,1,0:T(2,128)(2,1)S(1)} collective-permute-done((bf16[16,1,128]{2,1,0:T(2,128)(2,1)S(1)}, bf16[16,1,128]{2,1,0:T(2,128)(2,1)S(1)}, u32[]{:S(2)}, u32[]{:S(2)}) %collective-permute-start.1) | collective-permute-done | bytes 4128 | tf_op jit(solution)/shard_map/ppermute | solution.py:22
  57.4 0.4 multiply_reduce_fusion
  57.8 80.7 %all-gather.3.cloned.1.call-done = bf16[2048,3072]{1,0:T(8,128)(2,1)} async-done(((bf16[64,3072]{1,0:T(8,128)(2,1)}), bf16[2048,3072]{1,0:T(8,128)(2,1)}) %all-gather.3.cloned.1.call-update) | async-done | bytes 12582928 | tf_op jit(solution)/shard_map/all_gather | solution.py:59
  138.5 6.5 %convolution_convert_fusion.1 = bf16[128,3072]{1,0:T(8,128)(2,1)S(1)} fusion(bf16[2048,3072]{1,0:T(8,128)(2,1)} %all-gather.3.cloned.1.call-done, f32[128,2048]{1,0:T(8,128)S(1)} %get-tuple-element.72, f32[2048]{0:T(1024)S(1)} %copy-done.4, f32[128]{0:T(128)S(1)} %add_rsqrt_fusion), kind=kOutput, calls=%fused_computation.19 | convolution fusion | flops 1611792384 | bytes 14426624 | tf_op jit(solution)/shard_map/dot_general | solution.py:57
  145.0 2.9 %collective-permute-start.2 = (bf16[128,2048]{1,0:T(8,128)(2,1)S(1)}, bf16[128,2048]{1,0:T(8,128)(2,1)S(1)}, u32[]{:S(2)}, u32[]{:S(2)}) collective-permute-start(bf16[128,2048]{1,0:T(8,128)(2,1)S(1)} %slice.47), channel_id=1, source_target_pairs={{0,16},{16,32},{32,48},{48,64},{64,80},{80,96},{96,112},{112,128},... | collective-permute-start | bytes 1572872 | tf_op jit(solution)/shard_map/ppermute | solution.py:30
  148.1 1.9 collective-permute-start.4
  150.1 4.0 %collective-permute-done.2 = bf16[128,2048]{1,0:T(8,128)(2,1)S(1)} collective-permute-done((bf16[128,2048]{1,0:T(8,128)(2,1)S(1)}, bf16[128,2048]{1,0:T(8,128)(2,1)S(1)}, u32[]{:S(2)}, u32[]{:S(2)}) %collective-permute-start.2) | collective-permute-done | bytes 524320 | tf_op jit(solution)/shard_map/ppermute | solution.py:30
  154.1 4.4 %collective-permute-start.3 = (bf16[128,2048]{1,0:T(8,128)(2,1)S(1)}, bf16[128,2048]{1,0:T(8,128)(2,1)S(1)}, u32[]{:S(2)}, u32[]{:S(2)}) collective-permute-start(bf16[128,2048]{1,0:T(8,128)(2,1)S(1)} %collective-permute-done.2), channel_id=1, source_target_pairs={{0,16},{16,32},{32,48},{48,64},{64,80},{80,96},{96,112},{112,128},... | collective-permute-start | bytes 1572872 | tf_op jit(solution)/shard_map/ppermute | solution.py:30
  158.6 3.1 %collective-permute-done.4 = bf16[128,2048]{1,0:T(8,128)(2,1)S(1)} collective-permute-done((bf16[128,2048]{1,0:T(8,128)(2,1)S(1)}, bf16[128,2048]{1,0:T(8,128)(2,1)S(1)}, u32[]{:S(2)}, u32[]{:S(2)}) %collective-permute-start.4) | collective-permute-done | bytes 524320 | tf_op jit(solution)/shard_map/ppermute | solution.py:30
  161.7 1.9 collective-permute-start.5
  163.6 0.9 collective-permute-done.3
  164.7 11.3 %collective-permute-done.5 = bf16[128,2048]{1,0:T(8,128)(2,1)S(1)} collective-permute-done((bf16[128,2048]{1,0:T(8,128)(2,1)S(1)}, bf16[128,2048]{1,0:T(8,128)(2,1)S(1)}, u32[]{:S(2)}, u32[]{:S(2)}) %collective-permute-start.5) | collective-permute-done | bytes 524320 | tf_op jit(solution)/shard_map/ppermute | solution.py:30
  176.1 0.7 slice_bitcast_fusion
  176.8 0.6 bitcast_bitcast_fusion
  177.4 0.3 copy-done.3
  177.7 6.6 %while.11 = (s32[]{:T(128)}, bf16[8,128,128]{2,1,0:T(8,128)(2,1)S(1)}, bf16[8,128,128]{2,1,0:T(8,128)(2,1)S(1)}, bf16[8,640,128]{2,1,0:T(8,128)(2,1)S(1)}, bf16[...) while((s32[]{:T(128)}, bf16[8,128,128]{2,1,0:T(8,128)(2,1)S(1)}, ...), condition=%wide.region_5.6_spmd.clone, body=%wide.region_2.5_spmd.clone.sunk | while | flops 42614528 | bytes 1381965 | solution.py:88
  177.7 0.3 fusion.44
  178.6 0.3 fusion.44
  179.4 0.3 fusion.44
  184.5 0.8 reshape.99
  (52 shorter events, 7.1 us)
Async XLA Ops:
  6.5 44.2 %copy-start.2 = (bf16[16,8,128]{2,1,0:T(8,128)(2,1)S(1)}, bf16[16,8,128]{2,1,0:T(8,128)(2,1)}, u32[]{:S(2)}) copy-start(bf16[16,8,128]{2,1,0:T(8,128)(2,1)} %param.8) | copy-start | bytes 98308
  6.5 46.9 %copy-start = (bf16[3,128,2048]{2,1,0:T(8,128)(2,1)S(1)}, bf16[3,128,2048]{2,1,0:T(8,128)(2,1)}, u32[]{:S(2)}) copy-start(bf16[3,128,2048]{2,1,0:T(8,128)(2,1)} %param.10) | copy-start | bytes 4718596
  6.5 132.0 %all-gather.3.cloned.1.call-start = ((), (), s32[]{:S(2)}) async-start(), calls=%async_computation | async-start | bytes 12976128 | tf_op jit(solution)/shard_map/all_gather | solution.py:59
  49.4 4.3 %copy-start.1 = (bf16[16,8,2048]{2,1,0:T(8,128)(2,1)S(1)}, bf16[16,8,2048]{2,1,0:T(8,128)(2,1)}, u32[]{:S(2)}) copy-start(bf16[16,8,2048]{2,1,0:T(8,128)(2,1)} %param.9) | copy-start | bytes 1572868
  50.8 2.9 %collective-permute-start = (bf16[16,1,128]{2,1,0:T(2,128)(2,1)S(1)}, bf16[16,1,128]{2,1,0:T(2,128)(2,1)S(1)}, u32[]{:S(2)}, u32[]{:S(2)}) collective-permute-start(bf16[16,1,128]{2,1,0:T(2,128)(2,1)S(1)} %get-tuple-element.70), channel_id=1, source_target_pairs={{0,1},{1,2},{2,3},{3,4},{4,5},{5,6},{6,7},{7,8},{8,9},{9,10},{10,1... | collective-permute-start | bytes 12296 | tf_op jit(solution)/shard_map/ppermute | solution.py:21
  52.1 5.3 %collective-permute-start.1 = (bf16[16,1,128]{2,1,0:T(2,128)(2,1)S(1)}, bf16[16,1,128]{2,1,0:T(2,128)(2,1)S(1)}, u32[]{:S(2)}, u32[]{:S(2)}) collective-permute-start(bf16[16,1,128]{2,1,0:T(2,128)(2,1)S(1)} %get-tuple-element.69), channel_id=1, source_target_pairs={{1,0},{2,1},{3,2},{4,3},{5,4},{6,5},{7,6},{8,7},{9,8},{10,9},{11,1... | collective-permute-start | bytes 12296 | tf_op jit(solution)/shard_map/ppermute | solution.py:22
  54.0 84.5 %copy-start.4 = (f32[2048]{0:T(1024)S(1)}, f32[2048]{0:T(1024)}, u32[]{:S(2)}) copy-start(f32[2048]{0:T(1024)} %param.11) | copy-start | bytes 24580
  138.5 9.4 %copy-start.5 = (s32[1,1,5]{2,1,0:T(1,128)S(1)}, s32[1,1,5]{2,1,0:T(1,128)}, u32[]{:S(2)}) copy-start(s32[1,1,5]{2,1,0:T(1,128)} %param.13) | copy-start | bytes 64
  145.0 9.0 %collective-permute-start.2 = (bf16[128,2048]{1,0:T(8,128)(2,1)S(1)}, bf16[128,2048]{1,0:T(8,128)(2,1)S(1)}, u32[]{:S(2)}, u32[]{:S(2)}) collective-permute-start(bf16[128,2048]{1,0:T(8,128)(2,1)S(1)} %slice.47), channel_id=1, source_target_pairs={{0,16},{16,32},{32,48},{48,64},{64,80},{80,96},{96,112},{112,128},... | collective-permute-start | bytes 1572872 | tf_op jit(solution)/shard_map/ppermute | solution.py:30
  148.1 13.5 %collective-permute-start.4 = (bf16[128,2048]{1,0:T(8,128)(2,1)S(1)}, bf16[128,2048]{1,0:T(8,128)(2,1)S(1)}, u32[]{:S(2)}, u32[]{:S(2)}) collective-permute-start(bf16[128,2048]{1,0:T(8,128)(2,1)S(1)} %slice.47), channel_id=1, source_target_pairs={{16,0},{32,16},{48,32},{64,48},{80,64},{96,80},{112,96},{128,112},... | collective-permute-start | bytes 1572872 | tf_op jit(solution)/shard_map/ppermute | solution.py:30
  154.1 10.5 %collective-permute-start.3 = (bf16[128,2048]{1,0:T(8,128)(2,1)S(1)}, bf16[128,2048]{1,0:T(8,128)(2,1)S(1)}, u32[]{:S(2)}, u32[]{:S(2)}) collective-permute-start(bf16[128,2048]{1,0:T(8,128)(2,1)S(1)} %collective-permute-done.2), channel_id=1, source_target_pairs={{0,16},{16,32},{32,48},{48,64},{64,80},{80,96},{96,112},{112,128},... | collective-permute-start | bytes 1572872 | tf_op jit(solution)/shard_map/ppermute | solution.py:30
  161.7 14.4 %collective-permute-start.5 = (bf16[128,2048]{1,0:T(8,128)(2,1)S(1)}, bf16[128,2048]{1,0:T(8,128)(2,1)S(1)}, u32[]{:S(2)}, u32[]{:S(2)}) collective-permute-start(bf16[128,2048]{1,0:T(8,128)(2,1)S(1)} %collective-permute-done.4), channel_id=1, source_target_pairs={{16,0},{32,16},{48,32},{64,48},{80,64},{96,80},{112,96},{128,112},... | collective-permute-start | bytes 1572872 | tf_op jit(solution)/shard_map/ppermute | solution.py:30
  176.8 1.0 copy-start.3
Sparse Core Ops, SparseCore 0:
  50.9 87.5 all-gather.2
where the time goes:
time: 192 us
  waiting for transfers between devices  103 us (54%)
  blocking collectives  42.6 us (22%)
  starting transfers between devices  13.7 us (7%)
  between operations  13.6 us (7%)
  matrix products  12.1 us (6%)
  local copies, waits for them, and re-layouts  4.61 us (2%)
    all_gather x1, waiting for transfers between devices, per_device(): lax.all_gather(columns, 'tm', axis=0, tiled=True)  80.7 us
    all_gather x1, blocking collectives, per_device(): columns = lax.all_gather(w_qkv, 'depth', axis=1, tiled=True)  42.6 us
    ppermute x4, waiting for transfers between devices, from_behind(): return lax.ppermute(value, axis, pairs)  19.3 us
    ppermute x4, starting transfers between devices, from_behind(): return lax.ppermute(value, axis, pairs)  11.1 us
    dot_general x1, matrix products, per_device(): jnp.dot(normed, lax.all_gather(columns, 'tm', axis=0, tiled=True), prefer...  6.45 us
  transfers between devices with their start and end apart: 7, of which 6 were waited for; matrix products, arithmetic and copies ran while one was open for 1% of the time, Pallas kernels for 0%

commit v1 on v0

--- a/solution.py
+++ b/solution.py
@@ -53,7 +53,9 @@
     normed = (
         embedded * lax.rsqrt(jnp.mean(embedded * embedded, axis=-1, keepdims=True) + 1e-05) * gain
     ).astype(jnp.bfloat16)
-    columns = lax.all_gather(w_qkv, "depth", axis=1, tiled=True)
+    columns = jnp.concatenate(
+        lax.all_to_all(jnp.stack([w_qkv] * lax.axis_size("depth")), "depth", 0, 0), axis=1
+    )
     projected = jnp.dot(
         normed,
         lax.all_gather(columns, "tm", axis=0, tiled=True),

time: 192 us -> 174 us (0.906)
  blocking collectives: 42.6 us -> 27.4 us
  waiting for transfers between devices: 103 us -> 97 us
  starting transfers between devices: 13.7 us -> 16.1 us
    all_gather x1 -> x0, blocking collectives: 42.6 us -> none  [per_device(): columns = lax.all_gather(w_qkv, 'depth', axis=1, tiled=True)]
    all_to_all x0 -> x1, blocking collectives: none -> 27.4 us  [per_device(): lax.all_to_all(jnp.stack([w_qkv] * lax.axis_size('depth')), 'depth', 0, 0)]
    all_gather x1, waiting for transfers between devices: 80.7 us -> 74.4 us  [per_device(): lax.all_gather(columns, 'tm', axis=0, tiled=True)]
    ppermute x1, starting transfers between devices: 1.29 us -> 3.6 us  [padded_2(): before = lax.ppermute(last, axis, up)]
where the time goes in v1:
time: 174 us
  waiting for transfers between devices  97 us (56%)
  blocking collectives  27.4 us (16%)
  starting transfers between devices  16.1 us (9%)
  between operations  13.7 us (8%)
  matrix products  12.1 us (7%)
  local copies, waits for them, and re-layouts  5.41 us (3%)
  other arithmetic  1.87 us (1%)
    all_gather x1, waiting for transfers between devices, per_device(): lax.all_gather(columns, 'tm', axis=0, tiled=True)  74.4 us
    all_to_all x1, blocking collectives, per_device(): lax.all_to_all(jnp.stack([w_qkv] * lax.axis_size('depth')), 'depth', 0, 0)  27.4 us
    ppermute x4, waiting for transfers between devices, from_behind(): return lax.ppermute(value, axis, pairs)  19.3 us
    ppermute x4, starting transfers between devices, from_behind(): return lax.ppermute(value, axis, pairs)  11.2 us
    dot_general x1, matrix products, per_device(): jnp.dot(normed, lax.all_gather(columns, 'tm', axis=0, tiled=True), prefer...  6.45 us
    ppermute x1, starting transfers between devices, padded_2(): before = lax.ppermute(last, axis, up)  3.6 us
  transfers between devices with their start and end apart: 7, of which 6 were waited for; matrix products, arithmetic and copies ran while one was open for 1% of the time, Pallas kernels for 0%

profile of v1, /device:TPU:1, one launch (start us, length us, event | category | flops | bytes accessed | tf_op | source)
XLA Modules:
  0.0 173.8 jit_solution(15164344969350926737)
XLA Ops:
  6.5 0.8 stack.2
  7.4 27.4 %all_to_all.5 = bf16[16,64,192]{2,1,0:T(8,128)(2,1)S(1)} all-to-all(bf16[16,64,192]{2,1,0:T(8,128)(2,1)S(1)} %stack.2), channel_id=1, replica_groups=mesh['tm'=32,'depth'=16] {'depth'}, dimensions={0} | all-to-all | bytes 786432 | tf_op jit(solution)/shard_map/all_to_all | solution.py:57
  35.1 1.3 reshape.105
  36.4 3.6 %collective-permute-start = (bf16[16,1,128]{2,1,0:T(2,128)(2,1)S(1)}, bf16[16,1,128]{2,1,0:T(2,128)(2,1)S(1)}, u32[]{:S(2)}, u32[]{:S(2)}) collective-permute-start(bf16[16,1,128]{2,1,0:T(2,128)(2,1)S(1)} %get-tuple-element.70), channel_id=1, source_target_pairs={{0,1},{1,2},{2,3},{3,4},{4,5},{5,6},{6,7},{7,8},{8,9},{9,10},{10,1... | collective-permute-start | bytes 12296 | tf_op jit(solution)/shard_map/ppermute | solution.py:21
  40.0 1.3 collective-permute-start.1
  42.0 3.4 %collective-permute-done.1 = bf16[16,1,128]{2,1,0:T(2,128)(2,1)S(1)} collective-permute-done((bf16[16,1,128]{2,1,0:T(2,128)(2,1)S(1)}, bf16[16,1,128]{2,1,0:T(2,128)(2,1)S(1)}, u32[]{:S(2)}, u32[]{:S(2)}) %collective-permute-start.1) | collective-permute-done | bytes 4128 | tf_op jit(solution)/shard_map/ppermute | solution.py:22
  45.3 0.4 multiply_reduce_fusion
  45.7 74.4 %all-gather.2.cloned.1.call-done = bf16[2048,3072]{1,0:T(8,128)(2,1)} async-done(((bf16[64,3072]{1,0:T(8,128)(2,1)}), bf16[2048,3072]{1,0:T(8,128)(2,1)}) %all-gather.2.cloned.1.call-update) | async-done | bytes 12582928 | tf_op jit(solution)/shard_map/all_gather | solution.py:61
  120.1 6.5 %convolution_convert_fusion.1 = bf16[128,3072]{1,0:T(8,128)(2,1)S(1)} fusion(bf16[2048,3072]{1,0:T(8,128)(2,1)} %all-gather.2.cloned.1.call-done, f32[128,2048]{1,0:T(8,128)S(1)} %get-tuple-element.72, f32[2048]{0:T(1024)S(1)} %copy-done.4, f32[128]{0:T(128)S(1)} %add_rsqrt_fusion), kind=kOutput, calls=%fused_computation.19 | convolution fusion | flops 1611792384 | bytes 14426624 | tf_op jit(solution)/shard_map/dot_general | solution.py:59
  126.6 3.0 %collective-permute-start.2 = (bf16[128,2048]{1,0:T(8,128)(2,1)S(1)}, bf16[128,2048]{1,0:T(8,128)(2,1)S(1)}, u32[]{:S(2)}, u32[]{:S(2)}) collective-permute-start(bf16[128,2048]{1,0:T(8,128)(2,1)S(1)} %slice.47), channel_id=1, source_target_pairs={{0,16},{16,32},{32,48},{48,64},{64,80},{80,96},{96,112},{112,128},... | collective-permute-start | bytes 1572872 | tf_op jit(solution)/shard_map/ppermute | solution.py:30
  129.8 1.9 %collective-permute-start.4 = (bf16[128,2048]{1,0:T(8,128)(2,1)S(1)}, bf16[128,2048]{1,0:T(8,128)(2,1)S(1)}, u32[]{:S(2)}, u32[]{:S(2)}) collective-permute-start(bf16[128,2048]{1,0:T(8,128)(2,1)S(1)} %slice.47), channel_id=1, source_target_pairs={{16,0},{32,16},{48,32},{64,48},{80,64},{96,80},{112,96},{128,112},... | collective-permute-start | bytes 1572872 | tf_op jit(solution)/shard_map/ppermute | solution.py:30
  131.7 4.0 %collective-permute-done.2 = bf16[128,2048]{1,0:T(8,128)(2,1)S(1)} collective-permute-done((bf16[128,2048]{1,0:T(8,128)(2,1)S(1)}, bf16[128,2048]{1,0:T(8,128)(2,1)S(1)}, u32[]{:S(2)}, u32[]{:S(2)}) %collective-permute-start.2) | collective-permute-done | bytes 524320 | tf_op jit(solution)/shard_map/ppermute | solution.py:30
  135.7 4.4 %collective-permute-start.3 = (bf16[128,2048]{1,0:T(8,128)(2,1)S(1)}, bf16[128,2048]{1,0:T(8,128)(2,1)S(1)}, u32[]{:S(2)}, u32[]{:S(2)}) collective-permute-start(bf16[128,2048]{1,0:T(8,128)(2,1)S(1)} %collective-permute-done.2), channel_id=1, source_target_pairs={{0,16},{16,32},{32,48},{48,64},{64,80},{80,96},{96,112},{112,128},... | collective-permute-start | bytes 1572872 | tf_op jit(solution)/shard_map/ppermute | solution.py:30
  140.3 3.1 %collective-permute-done.4 = bf16[128,2048]{1,0:T(8,128)(2,1)S(1)} collective-permute-done((bf16[128,2048]{1,0:T(8,128)(2,1)S(1)}, bf16[128,2048]{1,0:T(8,128)(2,1)S(1)}, u32[]{:S(2)}, u32[]{:S(2)}) %collective-permute-start.4) | collective-permute-done | bytes 524320 | tf_op jit(solution)/shard_map/ppermute | solution.py:30
  143.3 1.9 %collective-permute-start.5 = (bf16[128,2048]{1,0:T(8,128)(2,1)S(1)}, bf16[128,2048]{1,0:T(8,128)(2,1)S(1)}, u32[]{:S(2)}, u32[]{:S(2)}) collective-permute-start(bf16[128,2048]{1,0:T(8,128)(2,1)S(1)} %collective-permute-done.4), channel_id=1, source_target_pairs={{16,0},{32,16},{48,32},{64,48},{80,64},{96,80},{112,96},{128,112},... | collective-permute-start | bytes 1572872 | tf_op jit(solution)/shard_map/ppermute | solution.py:30
  145.2 1.0 collective-permute-done.3
  146.4 11.2 %collective-permute-done.5 = bf16[128,2048]{1,0:T(8,128)(2,1)S(1)} collective-permute-done((bf16[128,2048]{1,0:T(8,128)(2,1)S(1)}, bf16[128,2048]{1,0:T(8,128)(2,1)S(1)}, u32[]{:S(2)}, u32[]{:S(2)}) %collective-permute-start.5) | collective-permute-done | bytes 524320 | tf_op jit(solution)/shard_map/ppermute | solution.py:30
  157.7 0.7 slice_bitcast_fusion
  158.4 0.6 bitcast_bitcast_fusion
  159.0 0.3 copy-done.3
  159.3 6.6 %while.11 = (s32[]{:T(128)}, bf16[8,128,128]{2,1,0:T(8,128)(2,1)S(1)}, bf16[8,128,128]{2,1,0:T(8,128)(2,1)S(1)}, bf16[8,640,128]{2,1,0:T(8,128)(2,1)S(1)}, bf16[...) while((s32[]{:T(128)}, bf16[8,128,128]{2,1,0:T(8,128)(2,1)S(1)}, ...), condition=%wide.region_5.6_spmd.clone, body=%wide.region_2.5_spmd.clone.sunk | while | flops 42614528 | bytes 1381965 | solution.py:90
  160.2 0.3 fusion.44
  161.0 0.3 fusion.44
  166.1 0.8 reshape.109
  (53 shorter events, 7.4 us)
Async XLA Ops:
  6.5 113.5 %all-gather.2.cloned.1.call-start = ((), (), s32[]{:S(2)}) async-start(), calls=%async_computation.1 | async-start | bytes 12976128 | tf_op jit(solution)/shard_map/all_gather | solution.py:61
  7.3 29.1 %copy-start.2 = (bf16[16,8,128]{2,1,0:T(8,128)(2,1)S(1)}, bf16[16,8,128]{2,1,0:T(8,128)(2,1)}, u32[]{:S(2)}) copy-start(bf16[16,8,128]{2,1,0:T(8,128)(2,1)} %param.8) | copy-start | bytes 98308
  7.4 34.0 %copy-start = (bf16[3,128,2048]{2,1,0:T(8,128)(2,1)S(1)}, bf16[3,128,2048]{2,1,0:T(8,128)(2,1)}, u32[]{:S(2)}) copy-start(bf16[3,128,2048]{2,1,0:T(8,128)(2,1)} %param.10) | copy-start | bytes 4718596
  35.0 6.6 %copy-start.1 = (bf16[16,8,2048]{2,1,0:T(8,128)(2,1)S(1)}, bf16[16,8,2048]{2,1,0:T(8,128)(2,1)}, u32[]{:S(2)}) copy-start(bf16[16,8,2048]{2,1,0:T(8,128)(2,1)} %param.9) | copy-start | bytes 1572868
  36.4 5.2 %collective-permute-start = (bf16[16,1,128]{2,1,0:T(2,128)(2,1)S(1)}, bf16[16,1,128]{2,1,0:T(2,128)(2,1)S(1)}, u32[]{:S(2)}, u32[]{:S(2)}) collective-permute-start(bf16[16,1,128]{2,1,0:T(2,128)(2,1)S(1)} %get-tuple-element.70), channel_id=1, source_target_pairs={{0,1},{1,2},{2,3},{3,4},{4,5},{5,6},{6,7},{7,8},{8,9},{9,10},{10,1... | collective-permute-start | bytes 12296 | tf_op jit(solution)/shard_map/ppermute | solution.py:21
  40.0 5.3 %collective-permute-start.1 = (bf16[16,1,128]{2,1,0:T(2,128)(2,1)S(1)}, bf16[16,1,128]{2,1,0:T(2,128)(2,1)S(1)}, u32[]{:S(2)}, u32[]{:S(2)}) collective-permute-start(bf16[16,1,128]{2,1,0:T(2,128)(2,1)S(1)} %get-tuple-element.69), channel_id=1, source_target_pairs={{1,0},{2,1},{3,2},{4,3},{5,4},{6,5},{7,6},{8,7},{9,8},{10,9},{11,1... | collective-permute-start | bytes 12296 | tf_op jit(solution)/shard_map/ppermute | solution.py:22
  42.0 78.1 %copy-start.4 = (f32[2048]{0:T(1024)S(1)}, f32[2048]{0:T(1024)}, u32[]{:S(2)}) copy-start(f32[2048]{0:T(1024)} %param.11) | copy-start | bytes 24580
  120.1 9.6 %copy-start.5 = (s32[1,1,5]{2,1,0:T(1,128)S(1)}, s32[1,1,5]{2,1,0:T(1,128)}, u32[]{:S(2)}) copy-start(s32[1,1,5]{2,1,0:T(1,128)} %param.13) | copy-start | bytes 64
  126.6 9.2 %collective-permute-start.2 = (bf16[128,2048]{1,0:T(8,128)(2,1)S(1)}, bf16[128,2048]{1,0:T(8,128)(2,1)S(1)}, u32[]{:S(2)}, u32[]{:S(2)}) collective-permute-start(bf16[128,2048]{1,0:T(8,128)(2,1)S(1)} %slice.47), channel_id=1, source_target_pairs={{0,16},{16,32},{32,48},{48,64},{64,80},{80,96},{96,112},{112,128},... | collective-permute-start | bytes 1572872 | tf_op jit(solution)/shard_map/ppermute | solution.py:30
  129.8 13.5 %collective-permute-start.4 = (bf16[128,2048]{1,0:T(8,128)(2,1)S(1)}, bf16[128,2048]{1,0:T(8,128)(2,1)S(1)}, u32[]{:S(2)}, u32[]{:S(2)}) collective-permute-start(bf16[128,2048]{1,0:T(8,128)(2,1)S(1)} %slice.47), channel_id=1, source_target_pairs={{16,0},{32,16},{48,32},{64,48},{80,64},{96,80},{112,96},{128,112},... | collective-permute-start | bytes 1572872 | tf_op jit(solution)/shard_map/ppermute | solution.py:30
  135.7 10.5 %collective-permute-start.3 = (bf16[128,2048]{1,0:T(8,128)(2,1)S(1)}, bf16[128,2048]{1,0:T(8,128)(2,1)S(1)}, u32[]{:S(2)}, u32[]{:S(2)}) collective-permute-start(bf16[128,2048]{1,0:T(8,128)(2,1)S(1)} %collective-permute-done.2), channel_id=1, source_target_pairs={{0,16},{16,32},{32,48},{48,64},{64,80},{80,96},{96,112},{112,128},... | collective-permute-start | bytes 1572872 | tf_op jit(solution)/shard_map/ppermute | solution.py:30
  143.3 14.3 %collective-permute-start.5 = (bf16[128,2048]{1,0:T(8,128)(2,1)S(1)}, bf16[128,2048]{1,0:T(8,128)(2,1)S(1)}, u32[]{:S(2)}, u32[]{:S(2)}) collective-permute-start(bf16[128,2048]{1,0:T(8,128)(2,1)S(1)} %collective-permute-done.4), channel_id=1, source_target_pairs={{16,0},{32,16},{48,32},{64,48},{80,64},{96,80},{112,96},{128,112},... | collective-permute-start | bytes 1572872 | tf_op jit(solution)/shard_map/ppermute | solution.py:30
  158.4 1.0 copy-start.3
Sparse Core Ops, SparseCore 0:
  36.5 83.5 all-gather.1
